TPU v7x, 128 devices: a whole 4x4x4 slice. The times are simulated.
128 devices in a mesh: dp: 64 (over y, z_hi, x, core), mp: 2 (over z_lo).
Axes of the slice: x: 4, y: 4, z: 4 (z_hi: 2, z_lo: 2; z = z_hi * 2 + z_lo), core: 2. Of those that a mesh axis runs over, the one named last changes fastest.
Arguments:
- belief: bfloat16 [16384, 2652], P('dp'), may hold values from -6 to 6
- target_value: bfloat16 [16384, 1326], P('dp'), may hold values from -6 to 6
- counts: int32 [128], P('dp'), may hold values from 1 to 128, as said below
- w_first: bfloat16 [2652, 1536], P(None, 'mp'), may hold values from -0.125 to 0.125
- w_middle: bfloat16 [1536, 1536], P('mp'), may hold values from -0.15625 to 0.15625
- w_last: bfloat16 [1536, 1326], P(None, 'mp'), may hold values from -0.15625 to 0.15625
Outputs:
- grad_first: float32 [2652, 1536], P(None, ('mp', 'dp'))
- grad_middle: float32 [1536, 1536], P('mp', 'dp')
- grad_last: float32 [1536, 1326], P('dp', 'mp')
Inputs may be any that keep to these rules, and one draw needn't show every extreme that they name: `counts`: rows past a subgame's count in its block are padding with arbitrary values.
All inputs are finite; a program needn't handle non-finite values.
Results may differ from a plain program's by a relative error of at most 0.0089.
Values may be sent and summed in bfloat16 or wider, within the bound.
No kernel may reach another device: no remote copies, remote signals or barrier semaphores. Data moves between devices by JAX's collectives and lax.ppermute only.
A program may use at most 192 MiB of HBM per device.

v0:
```python
import jax
import jax.numpy as jnp
from jax import lax
from jax.sharding import Mesh
from jax.sharding import PartitionSpec as P

BLOCK = 128
PARAMS = 8469504
DP = ("dp_0", "dp_1", "dp_2", "dp_3")
DP_MP = ("dp_0", "dp_1", "dp_2", "dp_3", "mp")
MP_DP = ("mp", "dp_0", "dp_1", "dp_2", "dp_3")


def copy_for_each(shard, axis):
    size = lax.axis_size(axis)
    return lax.all_to_all(
        jnp.broadcast_to(shard[None], (size, *shard.shape)), axis, 0, 0, tiled=True
    )


def taken_together(shard, axis):
    return copy_for_each(shard, axis).astype(jnp.float32).sum(axis=0)


def cut_along(shard, dim, size):
    lengths = shard.shape
    blocks = shard.reshape(*lengths[:dim], size, lengths[dim] // size, *lengths[dim + 1 :])
    return jnp.moveaxis(blocks, dim, 0)


def sum_at_owner(shard, axis, dim):
    size = lax.axis_size(axis)
    blocks = lax.all_to_all(cut_along(shard, dim, size), axis, 0, 0, tiled=True)
    return jnp.sum(blocks.astype(jnp.float32), axis=0)


def one_axis_at_a_time(shard, axes):
    for axis in axes:
        shard = lax.psum(shard, axis)
    return shard


def silu_slope(pre_act):
    sigmoid_of = jax.nn.sigmoid(pre_act)
    return sigmoid_of * (1.0 + pre_act * (1.0 - sigmoid_of))


def rows_grads(belief, target_value, live_mask, w_first, w_middle, w_last):
    pre_first = jnp.dot(belief, w_first, preferred_element_type=jnp.float32)
    act_first = jax.nn.silu(pre_first).astype(jnp.bfloat16)
    partial_middle = jnp.dot(act_first, w_middle, preferred_element_type=jnp.float32)
    pre_middle = taken_together(partial_middle.astype(jnp.bfloat16), "mp").astype(jnp.float32)
    act_middle = jax.nn.silu(pre_middle).astype(jnp.bfloat16)
    predicted = jnp.dot(act_middle, w_last, preferred_element_type=jnp.float32)
    mismatch = predicted - target_value.astype(jnp.float32)
    slope_out = (jnp.clip(mismatch, -1.0, 1.0) * live_mask[:, None]).astype(jnp.bfloat16)
    raw_last = jnp.dot(act_middle.T, slope_out, preferred_element_type=jnp.float32)
    partial_back = jnp.dot(slope_out, w_last.T, preferred_element_type=jnp.float32)
    back_middle = taken_together(partial_back.astype(jnp.bfloat16), "mp").astype(jnp.float32)
    slope_middle = (back_middle * silu_slope(pre_middle)).astype(jnp.bfloat16)
    raw_middle = jnp.dot(act_first.T, slope_middle, preferred_element_type=jnp.float32)
    back_first = jnp.dot(slope_middle, w_middle.T, preferred_element_type=jnp.float32)
    slope_first = (back_first * silu_slope(pre_first)).astype(jnp.bfloat16)
    raw_first = jnp.dot(belief.T, slope_first, preferred_element_type=jnp.float32)
    return (raw_first, raw_middle, raw_last)


def per_device(belief, target_value, counts, w_first, w_middle, w_last):
    total_rows = belief.shape[0]
    own_width = w_last.shape[1]
    target_value = lax.dynamic_slice_in_dim(
        target_value, lax.axis_index("mp") * own_width, own_width, 1
    )
    live_rows = (counts[:, None] > jnp.arange(BLOCK, dtype=jnp.int32)[None, :]).reshape(total_rows)
    raw_first, raw_middle, raw_last = rows_grads(
        belief, target_value, live_rows.astype(jnp.float32), w_first, w_middle, w_last
    )
    shard_first, shard_middle = (
        sum_at_owner(raw_first.astype(jnp.bfloat16), DP, 1),
        sum_at_owner(raw_middle.astype(jnp.bfloat16), DP, 1),
    )
    shard_last = sum_at_owner(raw_last.astype(jnp.bfloat16), DP, 0)
    local_squares = (
        jnp.sum(shard_first * shard_first)
        + jnp.sum(shard_middle * shard_middle)
        + jnp.sum(shard_last * shard_last)
    )
    square_sum = one_axis_at_a_time(local_squares, DP_MP)
    norm_scale = lax.rsqrt(square_sum / PARAMS + 1e-06)
    return (shard_first * norm_scale, shard_middle * norm_scale, shard_last * norm_scale)


def solution(mesh):
    finer = Mesh(
        mesh.devices.reshape(4, 2, 4, 2, mesh.shape["mp"]), ("dp_0", "dp_1", "dp_2", "dp_3", "mp")
    )
    return jax.shard_map(
        per_device,
        mesh=finer,
        in_specs=(P(DP, None), P(DP, None), P(DP), P(None, "mp"), P("mp", None), P(None, "mp")),
        out_specs=(P(None, MP_DP), P("mp", DP), P(DP, "mp")),
        check_vma=False,
    )
```

profile of v0, /device:TPU:0, one launch (start us, length us, event | category | flops | bytes accessed | tf_op | source)
XLA Modules:
  0.0 262.5 jit_solution(7464437599135056884)
XLA Ops:
  0.6 4.0 %fusion.12 = f32[256,768]{1,0:T(8,128)S(1)} fusion(bf16[256,2652]{0,1:T(8,128)(2,1)} %param.6, bf16[2652,768]{1,0:T(8,128)(2,1)} %param.9), kind=kOutput, calls=%fused_computation.36 | convolution fusion | flops 1042808832 | bytes 6217728 | tf_op jit(solution)/shard_map/dot_general | solution.py:49
  7.7 4.7 %all-to-all-start = ((bf16[2,256,1536]{2,1,0:T(8,128)(2,1)}), bf16[2,256,1536]{2,1,0:T(8,128)(2,1)}, u32[]{:S(2)}, u32[]{:S(2)}) async-start(bf16[2,256,1536]{2,1,0:T(8,128)(2,1)} %broadcast_in_dim.4), calls=%async_computation | async-start | bytes 3145728 | tf_op jit(solution)/shard_map/all_to_all | solution.py:16
  12.5 19.8 %all-to-all-done = bf16[2,256,1536]{2,1,0:T(8,128)(2,1)} async-done(((bf16[2,256,1536]{2,1,0:T(8,128)(2,1)}), bf16[2,256,1536]{2,1,0:T(8,128)(2,1)}, u32[]{:S(2)}, u32[]{:S(2)}) %all-to-all-start) | async-done | bytes 1572896 | tf_op jit(solution)/shard_map/all_to_all | solution.py:16
  37.6 4.6 %all-to-all-start.1 = ((bf16[2,256,1536]{2,1,0:T(8,128)(2,1)}), bf16[2,256,1536]{2,1,0:T(8,128)(2,1)}, u32[]{:S(2)}, u32[]{:S(2)}) async-start(bf16[2,256,1536]{2,1,0:T(8,128)(2,1)} %broadcast_in_dim.5), calls=%async_computation.1 | async-start | bytes 3145728 | tf_op jit(solution)/shard_map/all_to_all | solution.py:16
  42.2 3.5 %convolution_convert_fusion.2 = bf16[1536,663]{0,1:T(8,128)(2,1)} fusion(bf16[256,663]{0,1:T(8,128)(2,1)S(1)} %fusion.4, f32[256,1536]{1,0:T(8,128)} %copy-done.1), kind=kOutput, calls=%fused_computation.6 | convolution fusion | flops 524388864 | bytes 3949056 | tf_op jit(solution)/shard_map/dot_general | solution.py:57
  45.7 4.1 %copy.14 = bf16[1536,663]{1,0:T(8,128)(2,1)} copy(bf16[1536,663]{0,1:T(8,128)(2,1)} %convolution_convert_fusion.2) | data formatting | bytes 4073472 | tf_op jit(solution)/shard_map/convert_element_type | solution.py:82
  49.9 11.3 %all-to-all-done.1 = bf16[2,256,1536]{2,1,0:T(8,128)(2,1)} async-done(((bf16[2,256,1536]{2,1,0:T(8,128)(2,1)}), bf16[2,256,1536]{2,1,0:T(8,128)(2,1)}, u32[]{:S(2)}, u32[]{:S(2)}) %all-to-all-start.1) | async-done | bytes 1572896 | tf_op jit(solution)/shard_map/all_to_all | solution.py:16
  61.2 11.0 %all-to-all-start.4 = ((bf16[64,24,663]{2,1,0:T(8,128)(2,1)}), bf16[64,24,663]{2,1,0:T(8,128)(2,1)}, u32[]{:S(2)}, u32[]{:S(2)}) async-start(bf16[64,24,663]{2,1,0:T(8,128)(2,1)} %bitcast.23), calls=%async_computation.4 | async-start | bytes 4718592 | tf_op jit(solution)/shard_map/all_to_all | solution.py:33
  75.3 2.3 convolution_convert_fusion.1
  77.6 4.3 %copy.13 = bf16[768,1536]{0,1:T(8,128)(2,1)} copy(bf16[768,1536]{1,0:T(8,128)(2,1)} %convolution_convert_fusion.1) | data formatting | bytes 4718592 | tf_op jit(solution)/shard_map/convert_element_type | solution.py:80
  81.9 23.4 %all-to-all-done.4 = bf16[64,24,663]{2,1,0:T(8,128)(2,1)} async-done(((bf16[64,24,663]{2,1,0:T(8,128)(2,1)}), bf16[64,24,663]{2,1,0:T(8,128)(2,1)}, u32[]{:S(2)}, u32[]{:S(2)}) %all-to-all-start.4) | async-done | bytes 2036768 | tf_op jit(solution)/shard_map/all_to_all | solution.py:33
  105.3 5.5 %all-to-all-start.3 = ((bf16[64,768,24]{1,2,0:T(8,128)(2,1)}), bf16[64,768,24]{1,2,0:T(8,128)(2,1)}, u32[]{:S(2)}, u32[]{:S(2)}) async-start(bf16[64,768,24]{1,2,0:T(8,128)(2,1)} %bitcast.24), calls=%async_computation.3 | async-start | bytes 4718592 | tf_op jit(solution)/shard_map/all_to_all | solution.py:33
  110.8 5.5 %fusion = bf16[2652,768]{1,0:T(8,128)(2,1)} fusion(bf16[256,2652]{0,1:T(8,128)(2,1)} %param.6, bf16[256,1536]{1,0:T(8,128)(2,1)S(1)} %multiply_convert_fusion, bf16[768,1536]{1,0:T(8,128)(2,1)S(1)} %copy-done, f32[256,768]{1,0:T(8,128)} %copy-done.6), kind=kOutput, calls=%fused_computation.4 | convolution fusion | flops 1650594816 | bytes 9363456 | tf_op jit(solution)/shard_map/dot_general | solution.py:64
  116.3 6.4 %copy.12 = bf16[2652,768]{0,1:T(8,128)(2,1)} copy(bf16[2652,768]{1,0:T(8,128)(2,1)} %fusion) | data formatting | bytes 8146944 | tf_op jit(solution)/shard_map/convert_element_type | solution.py:79
  122.7 7.1 %reshape.34 = bf16[2652,64,12]{0,2,1:T(8,128)(2,1)} reshape(bf16[2652,768]{0,1:T(8,128)(2,1)} %copy.12) | data formatting | bytes 8146944 | tf_op jit(solution)/shard_map/reshape | solution.py:27
  129.9 14.0 %all-to-all-done.3 = bf16[64,768,24]{1,2,0:T(8,128)(2,1)} async-done(((bf16[64,768,24]{1,2,0:T(8,128)(2,1)}), bf16[64,768,24]{1,2,0:T(8,128)(2,1)}, u32[]{:S(2)}, u32[]{:S(2)}) %all-to-all-start.3) | async-done | bytes 2359328 | tf_op jit(solution)/shard_map/all_to_all | solution.py:33
  143.9 5.9 %all-to-all-start.2 = ((bf16[64,2652,12]{1,2,0:T(8,128)(2,1)}), bf16[64,2652,12]{1,2,0:T(8,128)(2,1)}, u32[]{:S(2)}, u32[]{:S(2)}) async-start(bf16[64,2652,12]{1,2,0:T(8,128)(2,1)} %bitcast.22), calls=%async_computation.2 | async-start | bytes 11010048 | tf_op jit(solution)/shard_map/all_to_all | solution.py:33
  155.1 62.1 %all-to-all-done.2 = bf16[64,2652,12]{1,2,0:T(8,128)(2,1)} async-done(((bf16[64,2652,12]{1,2,0:T(8,128)(2,1)}), bf16[64,2652,12]{1,2,0:T(8,128)(2,1)}, u32[]{:S(2)}, u32[]{:S(2)}) %all-to-all-start.2) | async-done | bytes 4073504 | tf_op jit(solution)/shard_map/all_to_all | solution.py:33
  217.2 3.5 %convert_reduce_fusion = f32[2652,12]{0,1:T(8,128)S(1)} fusion(bf16[64,2652,12]{1,2,0:T(8,128)(2,1)} %all-to-all-done.2), kind=kLoop, calls=%fused_computation | loop fusion | flops 4041648 | bytes 4200768 | tf_op jit(solution)/shard_map/reduce_sum | solution.py:34
  223.3 10.2 %psum.35 = f32[]{:T(128)} all-reduce(f32[]{:T(128)S(6)} %add.44), channel_id=1, replica_groups=mesh['dp_0'=4,'dp_1'=2,'dp_2'=4,'dp_3'=2,'mp'=2] {'dp_0'}, use_global_device_ids=true, to_apply=%region_8.9 | all-reduce | flops 1 | bytes 8 | tf_op jit(solution)/shard_map/psum | solution.py:39
  233.5 7.1 %psum.36 = f32[]{:T(128)} all-reduce(f32[]{:T(128)} %psum.35), channel_id=1, replica_groups=mesh['dp_0'=4,'dp_1'=2,'dp_2'=4,'dp_3'=2,'mp'=2] {'dp_1'}, use_global_device_ids=true, to_apply=%region_9.10 | all-reduce | flops 1 | bytes 8 | tf_op jit(solution)/shard_map/psum | solution.py:39
  240.6 10.6 %psum.37 = f32[]{:T(128)} all-reduce(f32[]{:T(128)} %psum.36), channel_id=1, replica_groups=mesh['dp_0'=4,'dp_1'=2,'dp_2'=4,'dp_3'=2,'mp'=2] {'dp_2'}, use_global_device_ids=true, to_apply=%region_10.11 | all-reduce | flops 1 | bytes 8 | tf_op jit(solution)/shard_map/psum | solution.py:39
  251.2 3.1 %psum.38 = f32[]{:T(128)} all-reduce(f32[]{:T(128)} %psum.37), channel_id=1, replica_groups=mesh['dp_0'=4,'dp_1'=2,'dp_2'=4,'dp_3'=2,'mp'=2] {'dp_3'}, use_global_device_ids=true, to_apply=%region_11.12 | all-reduce | flops 1 | bytes 8 | tf_op jit(solution)/shard_map/psum | solution.py:39
  254.3 5.5 %psum.39 = f32[]{:T(128)} all-reduce(f32[]{:T(128)} %psum.38), channel_id=1, replica_groups=mesh['dp_0'=4,'dp_1'=2,'dp_2'=4,'dp_3'=2,'mp'=2] {'mp'}, use_global_device_ids=true, to_apply=%region_12.13 | all-reduce | flops 1 | bytes 8 | tf_op jit(solution)/shard_map/psum | solution.py:39
  (33 shorter events, 19.3 us)
Async XLA Ops:
  0.6 5.0 %copy-start = (bf16[768,1536]{1,0:T(8,128)(2,1)S(1)}, bf16[768,1536]{1,0:T(8,128)(2,1)}, u32[]{:S(2)}) copy-start(bf16[768,1536]{1,0:T(8,128)(2,1)} %param.10) | copy-start | bytes 7077892
  4.7 0.9 copy-start.6
  7.7 4.7 %copy-start.5 = (s32[2]{0:T(128)S(1)}, s32[2]{0:T(128)}, u32[]{:S(2)}) copy-start(s32[2]{0:T(128)} %param.8) | copy-start | bytes 28
  7.7 24.6 %all-to-all-start = ((bf16[2,256,1536]{2,1,0:T(8,128)(2,1)}), bf16[2,256,1536]{2,1,0:T(8,128)(2,1)}, u32[]{:S(2)}, u32[]{:S(2)}) async-start(bf16[2,256,1536]{2,1,0:T(8,128)(2,1)} %broadcast_in_dim.4), calls=%async_computation | async-start | bytes 3145728 | tf_op jit(solution)/shard_map/all_to_all | solution.py:16
  12.5 21.8 %copy-start.4 = (bf16[256,1326]{0,1:T(8,128)(2,1)S(1)}, bf16[256,1326]{0,1:T(8,128)(2,1)}, u32[]{:S(2)}) copy-start(bf16[256,1326]{0,1:T(8,128)(2,1)} %param.7) | copy-start | bytes 2036740
  32.3 2.0 copy-start.3
  34.3 1.1 copy-start.1
  37.6 23.6 %all-to-all-start.1 = ((bf16[2,256,1536]{2,1,0:T(8,128)(2,1)}), bf16[2,256,1536]{2,1,0:T(8,128)(2,1)}, u32[]{:S(2)}, u32[]{:S(2)}) async-start(bf16[2,256,1536]{2,1,0:T(8,128)(2,1)} %broadcast_in_dim.5), calls=%async_computation.1 | async-start | bytes 3145728 | tf_op jit(solution)/shard_map/all_to_all | solution.py:16
  61.2 44.1 %all-to-all-start.4 = ((bf16[64,24,663]{2,1,0:T(8,128)(2,1)}), bf16[64,24,663]{2,1,0:T(8,128)(2,1)}, u32[]{:S(2)}, u32[]{:S(2)}) async-start(bf16[64,24,663]{2,1,0:T(8,128)(2,1)} %bitcast.23), calls=%async_computation.4 | async-start | bytes 4718592 | tf_op jit(solution)/shard_map/all_to_all | solution.py:33
  72.2 2.0 copy-start.2
  74.2 1.1 copy-start.7
  105.3 38.6 %all-to-all-start.3 = ((bf16[64,768,24]{1,2,0:T(8,128)(2,1)}), bf16[64,768,24]{1,2,0:T(8,128)(2,1)}, u32[]{:S(2)}, u32[]{:S(2)}) async-start(bf16[64,768,24]{1,2,0:T(8,128)(2,1)} %bitcast.24), calls=%async_computation.3 | async-start | bytes 4718592 | tf_op jit(solution)/shard_map/all_to_all | solution.py:33
  143.9 73.3 %all-to-all-start.2 = ((bf16[64,2652,12]{1,2,0:T(8,128)(2,1)}), bf16[64,2652,12]{1,2,0:T(8,128)(2,1)}, u32[]{:S(2)}, u32[]{:S(2)}) async-start(bf16[64,2652,12]{1,2,0:T(8,128)(2,1)} %bitcast.22), calls=%async_computation.2 | async-start | bytes 11010048 | tf_op jit(solution)/shard_map/all_to_all | solution.py:33
where the time goes:
time: 264 us; the launch traced here: 262 us
  waiting for transfers between devices  131 us (50%)
  blocking collectives  36.5 us (14%)
  starting transfers between devices  31.7 us (12%)
  local copies, waits for them, and re-layouts  26.3 us (10%)
  matrix products  17.8 us (7%)
  other arithmetic  16 us (6%)
  between operations  3.43 us (1%)
    all_to_all x3, waiting for transfers between devices, sum_at_owner(): blocks = lax.all_to_all(cut_along(shard, dim, size), axis, 0, 0, tiled=True)  99.5 us
    psum x5, blocking collectives, one_axis_at_a_time(): shard = lax.psum(shard, axis)  36.5 us
    all_to_all x2, waiting for transfers between devices, copy_for_each(): lax.all_to_all(jnp.broadcast_to(shard[None], (size, *shard.shape)), axis,...  31.1 us
    all_to_all x3, starting transfers between devices, sum_at_owner(): blocks = lax.all_to_all(cut_along(shard, dim, size), axis, 0, 0, tiled=True)  22.4 us
    all_to_all x2, starting transfers between devices, copy_for_each(): lax.all_to_all(jnp.broadcast_to(shard[None], (size, *shard.shape)), axis,...  9.34 us
    reduce_sum x3, other arithmetic, sum_at_owner(): return jnp.sum(blocks.astype(jnp.float32), axis=0)  7.58 us
    reshape x1, local copies, waits for them, and re-layouts, cut_along(): shard.reshape(*lengths[:dim], size, lengths[dim] // size, *lengths[dim +...  7.11 us
    convert_element_type x1, local copies, waits for them, and re-layouts, per_device(): raw_first.astype(jnp.bfloat16)  6.42 us
  transfers between devices with their start and end apart: 5, of which 5 were waited for; matrix products, arithmetic and copies ran while one was open for 16% of the time, Pallas kernels for 0%

commit v1 on v0

--- a/solution.py
+++ b/solution.py
@@ -36,7 +36,7 @@
 
 def one_axis_at_a_time(shard, axes):
     for axis in axes:
-        shard = lax.psum(shard, axis)
+        shard = jnp.sum(lax.all_gather(shard, axis), axis=0)
     return shard
 
 

time: 264 us -> 273 us (1.034)
  local copies, waits for them, and re-layouts: 26.3 us -> 35.6 us
  blocking collectives: 36.5 us -> 33.4 us
  other arithmetic: 16 us -> 19 us
    psum x5 -> x0, blocking collectives: 36.5 us -> none  [one_axis_at_a_time(): shard = lax.psum(shard, axis)]
    unnamed x0 -> x5, blocking collectives: none -> 33.4 us
    unnamed x16 -> x41, local copies, waits for them, and re-layouts: 1.77 us -> 11.1 us
    reduce_sum x0 -> x5, other arithmetic: none -> 3.02 us  [one_axis_at_a_time(): shard = jnp.sum(lax.all_gather(shard, axis), axis=0)]
  transfers between devices with their start and end apart: 5 -> 5, of which waited for: 5 -> 5; matrix products, arithmetic and copies ran while one was open for 16% -> 15% of each run, Pallas kernels for 0% -> 0%
where the time goes in v1:
time: 273 us; the launch traced here: 271 us
  waiting for transfers between devices  130 us (48%)
  local copies, waits for them, and re-layouts  35.6 us (13%)
  blocking collectives  33.4 us (12%)
  starting transfers between devices  31.9 us (12%)
  other arithmetic  19 us (7%)
  matrix products  17.8 us (7%)
  between operations  3.47 us (1%)
    all_to_all x3, waiting for transfers between devices, sum_at_owner(): blocks = lax.all_to_all(cut_along(shard, dim, size), axis, 0, 0, tiled=True)  98.9 us
    unnamed x5, blocking collectives  33.4 us
    all_to_all x2, waiting for transfers between devices, copy_for_each(): lax.all_to_all(jnp.broadcast_to(shard[None], (size, *shard.shape)), axis,...  31.1 us
    all_to_all x3, starting transfers between devices, sum_at_owner(): blocks = lax.all_to_all(cut_along(shard, dim, size), axis, 0, 0, tiled=True)  22.5 us
    unnamed x41, local copies, waits for them, and re-layouts  11.1 us
    all_to_all x2, starting transfers between devices, copy_for_each(): lax.all_to_all(jnp.broadcast_to(shard[None], (size, *shard.shape)), axis,...  9.34 us
    reduce_sum x3, other arithmetic, sum_at_owner(): return jnp.sum(blocks.astype(jnp.float32), axis=0)  7.58 us
    reshape x1, local copies, waits for them, and re-layouts, cut_along(): shard.reshape(*lengths[:dim], size, lengths[dim] // size, *lengths[dim +...  7.11 us
  transfers between devices with their start and end apart: 5, of which 5 were waited for; matrix products, arithmetic and copies ran while one was open for 15% of the time, Pallas kernels for 0%

profile of v1, /device:TPU:0, one launch (start us, length us, event | category | flops | bytes accessed | tf_op | source)
XLA Modules:
  0.0 271.3 jit_solution(6612197896418310964)
XLA Ops:
  0.6 4.0 %fusion.12 = f32[256,768]{1,0:T(8,128)S(1)} fusion(bf16[256,2652]{0,1:T(8,128)(2,1)} %param.6, bf16[2652,768]{1,0:T(8,128)(2,1)} %param.9), kind=kOutput, calls=%fused_computation.36 | convolution fusion | flops 1042808832 | bytes 6217728 | tf_op jit(solution)/shard_map/dot_general | solution.py:49
  7.7 4.7 %all-to-all-start = ((bf16[2,256,1536]{2,1,0:T(8,128)(2,1)}), bf16[2,256,1536]{2,1,0:T(8,128)(2,1)}, u32[]{:S(2)}, u32[]{:S(2)}) async-start(bf16[2,256,1536]{2,1,0:T(8,128)(2,1)} %broadcast_in_dim.4), calls=%async_computation | async-start | bytes 3145728 | tf_op jit(solution)/shard_map/all_to_all | solution.py:16
  12.5 19.8 %all-to-all-done = bf16[2,256,1536]{2,1,0:T(8,128)(2,1)} async-done(((bf16[2,256,1536]{2,1,0:T(8,128)(2,1)}), bf16[2,256,1536]{2,1,0:T(8,128)(2,1)}, u32[]{:S(2)}, u32[]{:S(2)}) %all-to-all-start) | async-done | bytes 1572896 | tf_op jit(solution)/shard_map/all_to_all | solution.py:16
  37.6 4.6 %all-to-all-start.1 = ((bf16[2,256,1536]{2,1,0:T(8,128)(2,1)}), bf16[2,256,1536]{2,1,0:T(8,128)(2,1)}, u32[]{:S(2)}, u32[]{:S(2)}) async-start(bf16[2,256,1536]{2,1,0:T(8,128)(2,1)} %broadcast_in_dim.5), calls=%async_computation.1 | async-start | bytes 3145728 | tf_op jit(solution)/shard_map/all_to_all | solution.py:16
  42.2 3.5 %convolution_convert_fusion.2 = bf16[1536,663]{0,1:T(8,128)(2,1)} fusion(bf16[256,663]{0,1:T(8,128)(2,1)S(1)} %fusion.4, f32[256,1536]{1,0:T(8,128)} %copy-done.1), kind=kOutput, calls=%fused_computation.6 | convolution fusion | flops 524388864 | bytes 3949056 | tf_op jit(solution)/shard_map/dot_general | solution.py:57
  45.7 4.1 %copy.14 = bf16[1536,663]{1,0:T(8,128)(2,1)} copy(bf16[1536,663]{0,1:T(8,128)(2,1)} %convolution_convert_fusion.2) | data formatting | bytes 4073472 | tf_op jit(solution)/shard_map/convert_element_type | solution.py:82
  49.9 11.3 %all-to-all-done.1 = bf16[2,256,1536]{2,1,0:T(8,128)(2,1)} async-done(((bf16[2,256,1536]{2,1,0:T(8,128)(2,1)}), bf16[2,256,1536]{2,1,0:T(8,128)(2,1)}, u32[]{:S(2)}, u32[]{:S(2)}) %all-to-all-start.1) | async-done | bytes 1572896 | tf_op jit(solution)/shard_map/all_to_all | solution.py:16
  61.2 11.0 %all-to-all-start.4 = ((bf16[64,24,663]{2,1,0:T(8,128)(2,1)}), bf16[64,24,663]{2,1,0:T(8,128)(2,1)}, u32[]{:S(2)}, u32[]{:S(2)}) async-start(bf16[64,24,663]{2,1,0:T(8,128)(2,1)} %bitcast.33), calls=%async_computation.4 | async-start | bytes 4718592 | tf_op jit(solution)/shard_map/all_to_all | solution.py:33
  75.3 2.3 convolution_convert_fusion.1
  77.6 4.3 %copy.13 = bf16[768,1536]{0,1:T(8,128)(2,1)} copy(bf16[768,1536]{1,0:T(8,128)(2,1)} %convolution_convert_fusion.1) | data formatting | bytes 4718592 | tf_op jit(solution)/shard_map/convert_element_type | solution.py:80
  81.9 23.4 %all-to-all-done.4 = bf16[64,24,663]{2,1,0:T(8,128)(2,1)} async-done(((bf16[64,24,663]{2,1,0:T(8,128)(2,1)}), bf16[64,24,663]{2,1,0:T(8,128)(2,1)}, u32[]{:S(2)}, u32[]{:S(2)}) %all-to-all-start.4) | async-done | bytes 2036768 | tf_op jit(solution)/shard_map/all_to_all | solution.py:33
  105.3 5.5 %all-to-all-start.3 = ((bf16[64,768,24]{1,2,0:T(8,128)(2,1)}), bf16[64,768,24]{1,2,0:T(8,128)(2,1)}, u32[]{:S(2)}, u32[]{:S(2)}) async-start(bf16[64,768,24]{1,2,0:T(8,128)(2,1)} %bitcast.34), calls=%async_computation.3 | async-start | bytes 4718592 | tf_op jit(solution)/shard_map/all_to_all | solution.py:33
  110.8 5.5 %fusion = bf16[2652,768]{1,0:T(8,128)(2,1)} fusion(bf16[256,2652]{0,1:T(8,128)(2,1)} %param.6, bf16[256,1536]{1,0:T(8,128)(2,1)S(1)} %multiply_convert_fusion, bf16[768,1536]{1,0:T(8,128)(2,1)S(1)} %copy-done, f32[256,768]{1,0:T(8,128)} %copy-done.11), kind=kOutput, calls=%fused_computation.4 | convolution fusion | flops 1650594816 | bytes 9363456 | tf_op jit(solution)/shard_map/dot_general | solution.py:64
  116.3 6.4 %copy.12 = bf16[2652,768]{0,1:T(8,128)(2,1)} copy(bf16[2652,768]{1,0:T(8,128)(2,1)} %fusion) | data formatting | bytes 8146944 | tf_op jit(solution)/shard_map/convert_element_type | solution.py:79
  122.7 7.1 %reshape.34 = bf16[2652,64,12]{0,2,1:T(8,128)(2,1)} reshape(bf16[2652,768]{0,1:T(8,128)(2,1)} %copy.12) | data formatting | bytes 8146944 | tf_op jit(solution)/shard_map/reshape | solution.py:27
  129.9 14.0 %all-to-all-done.3 = bf16[64,768,24]{1,2,0:T(8,128)(2,1)} async-done(((bf16[64,768,24]{1,2,0:T(8,128)(2,1)}), bf16[64,768,24]{1,2,0:T(8,128)(2,1)}, u32[]{:S(2)}, u32[]{:S(2)}) %all-to-all-start.3) | async-done | bytes 2359328 | tf_op jit(solution)/shard_map/all_to_all | solution.py:33
  143.9 6.0 %all-to-all-start.2 = ((bf16[64,2652,12]{1,2,0:T(8,128)(2,1)}), bf16[64,2652,12]{1,2,0:T(8,128)(2,1)}, u32[]{:S(2)}, u32[]{:S(2)}) async-start(bf16[64,2652,12]{1,2,0:T(8,128)(2,1)} %bitcast.32), calls=%async_computation.2 | async-start | bytes 11010048 | tf_op jit(solution)/shard_map/all_to_all | solution.py:33
  155.8 61.5 %all-to-all-done.2 = bf16[64,2652,12]{1,2,0:T(8,128)(2,1)} async-done(((bf16[64,2652,12]{1,2,0:T(8,128)(2,1)}), bf16[64,2652,12]{1,2,0:T(8,128)(2,1)}, u32[]{:S(2)}, u32[]{:S(2)}) %all-to-all-start.2) | async-done | bytes 4073504 | tf_op jit(solution)/shard_map/all_to_all | solution.py:33
  217.3 3.5 %convert_reduce_fusion = f32[2652,12]{0,1:T(8,128)S(1)} fusion(bf16[64,2652,12]{1,2,0:T(8,128)(2,1)} %all-to-all-done.2), kind=kLoop, calls=%fused_computation | loop fusion | flops 4041648 | bytes 4200768 | tf_op jit(solution)/shard_map/reduce_sum | solution.py:34
  224.8 9.7 %all-reduce = f32[4]{0:T(128)S(1)} all-reduce(f32[4]{0:T(128)S(1)} %dynamic-update-slice), channel_id=1, replica_groups=mesh['dp_0'=4,'dp_1'=2,'dp_2'=4,'dp_3'=2,'mp'=2] {'dp_0'}, use_global_device_ids=true, to_apply=%add | all-reduce | flops 4 | bytes 32
  237.0 6.4 %all-reduce.1 = f32[2]{0:T(128)S(1)} all-reduce(f32[2]{0:T(128)S(1)} %dynamic-update-slice.1), channel_id=1, replica_groups=mesh['dp_0'=4,'dp_1'=2,'dp_2'=4,'dp_3'=2,'mp'=2] {'dp_1'}, use_global_device_ids=true, to_apply=%add.1 | all-reduce | flops 2 | bytes 16
  246.0 10.0 %all-reduce.2 = f32[4]{0:T(128)S(1)} all-reduce(f32[4]{0:T(128)S(1)} %dynamic-update-slice.2), channel_id=1, replica_groups=mesh['dp_0'=4,'dp_1'=2,'dp_2'=4,'dp_3'=2,'mp'=2] {'dp_2'}, use_global_device_ids=true, to_apply=%add.2 | all-reduce | flops 4 | bytes 32
  258.6 2.4 all-reduce.3
  263.1 4.9 %all-reduce.4 = f32[2]{0:T(128)S(1)} all-reduce(f32[2]{0:T(128)S(1)} %dynamic-update-slice.4), channel_id=1, replica_groups=mesh['dp_0'=4,'dp_1'=2,'dp_2'=4,'dp_3'=2,'mp'=2] {'mp'}, use_global_device_ids=true, to_apply=%add.4 | all-reduce | flops 2 | bytes 16
  (63 shorter events, 31.6 us)
Async XLA Ops:
  0.6 5.0 %copy-start = (bf16[768,1536]{1,0:T(8,128)(2,1)S(1)}, bf16[768,1536]{1,0:T(8,128)(2,1)}, u32[]{:S(2)}) copy-start(bf16[768,1536]{1,0:T(8,128)(2,1)} %param.10) | copy-start | bytes 7077892
  4.7 0.9 copy-start.11
  7.7 4.7 %copy-start.5 = (s32[2]{0:T(128)S(1)}, s32[2]{0:T(128)}, u32[]{:S(2)}) copy-start(s32[2]{0:T(128)} %param.8) | copy-start | bytes 28
  7.7 24.6 %all-to-all-start = ((bf16[2,256,1536]{2,1,0:T(8,128)(2,1)}), bf16[2,256,1536]{2,1,0:T(8,128)(2,1)}, u32[]{:S(2)}, u32[]{:S(2)}) async-start(bf16[2,256,1536]{2,1,0:T(8,128)(2,1)} %broadcast_in_dim.4), calls=%async_computation | async-start | bytes 3145728 | tf_op jit(solution)/shard_map/all_to_all | solution.py:16
  12.5 21.8 %copy-start.4 = (bf16[256,1326]{0,1:T(8,128)(2,1)S(1)}, bf16[256,1326]{0,1:T(8,128)(2,1)}, u32[]{:S(2)}) copy-start(bf16[256,1326]{0,1:T(8,128)(2,1)} %param.7) | copy-start | bytes 2036740
  32.3 2.0 copy-start.3
  34.3 1.1 copy-start.1
  37.6 23.6 %all-to-all-start.1 = ((bf16[2,256,1536]{2,1,0:T(8,128)(2,1)}), bf16[2,256,1536]{2,1,0:T(8,128)(2,1)}, u32[]{:S(2)}, u32[]{:S(2)}) async-start(bf16[2,256,1536]{2,1,0:T(8,128)(2,1)} %broadcast_in_dim.5), calls=%async_computation.1 | async-start | bytes 3145728 | tf_op jit(solution)/shard_map/all_to_all | solution.py:16
  61.2 44.1 %all-to-all-start.4 = ((bf16[64,24,663]{2,1,0:T(8,128)(2,1)}), bf16[64,24,663]{2,1,0:T(8,128)(2,1)}, u32[]{:S(2)}, u32[]{:S(2)}) async-start(bf16[64,24,663]{2,1,0:T(8,128)(2,1)} %bitcast.33), calls=%async_computation.4 | async-start | bytes 4718592 | tf_op jit(solution)/shard_map/all_to_all | solution.py:33
  72.2 2.0 copy-start.2
  74.2 1.1 copy-start.12
  105.3 38.6 %all-to-all-start.3 = ((bf16[64,768,24]{1,2,0:T(8,128)(2,1)}), bf16[64,768,24]{1,2,0:T(8,128)(2,1)}, u32[]{:S(2)}, u32[]{:S(2)}) async-start(bf16[64,768,24]{1,2,0:T(8,128)(2,1)} %bitcast.34), calls=%async_computation.3 | async-start | bytes 4718592 | tf_op jit(solution)/shard_map/all_to_all | solution.py:33
  143.9 6.0 %copy-start.10 = (u32[128]{0:T(128)S(1)}, u32[128]{0:T(128)}, u32[]{:S(2)}) copy-start(u32[128]{0:T(128)} %constant.31) | copy-start | bytes 1540
  143.9 73.4 %all-to-all-start.2 = ((bf16[64,2652,12]{1,2,0:T(8,128)(2,1)}), bf16[64,2652,12]{1,2,0:T(8,128)(2,1)}, u32[]{:S(2)}, u32[]{:S(2)}) async-start(bf16[64,2652,12]{1,2,0:T(8,128)(2,1)} %bitcast.32), calls=%async_computation.2 | async-start | bytes 11010048 | tf_op jit(solution)/shard_map/all_to_all | solution.py:33
  155.8 68.3 %copy-start.9 = (u32[128]{0:T(128)S(1)}, u32[128]{0:T(128)}, u32[]{:S(2)}) copy-start(u32[128]{0:T(128)} %constant.36) | copy-start | bytes 1540
  155.8 80.6 %copy-start.8 = (u32[128]{0:T(128)S(1)}, u32[128]{0:T(128)}, u32[]{:S(2)}) copy-start(u32[128]{0:T(128)} %constant.41) | copy-start | bytes 1540
  155.8 89.6 %copy-start.7 = (u32[128]{0:T(128)S(1)}, u32[128]{0:T(128)}, u32[]{:S(2)}) copy-start(u32[128]{0:T(128)} %constant.46) | copy-start | bytes 1540
  155.8 102.2 %copy-start.6 = (u32[128]{0:T(128)S(1)}, u32[128]{0:T(128)}, u32[]{:S(2)}) copy-start(u32[128]{0:T(128)} %constant.51) | copy-start | bytes 1540
